TPU v7x, 512 devices: a whole 4x4x16 slice. The times are simulated.
512 devices in a mesh: section: 2 (over y_hi), wide: 64 (over z, y_lo, core), narrow: 4 (over x).
Axes of the slice: x: 4, y: 4 (y_hi: 2, y_lo: 2; y = y_hi * 2 + y_lo), z: 16, core: 2. Of those that a mesh axis runs over, the one named last changes fastest.
Arguments:
- token_shard: int32 [16384, 1], P(('section', 'wide')), may hold values from 0 to 127; in each aligned block of 128 rows (0 to 127, 128 to 255, ...) at most 2 rows name the same one
- token_row: int32 [16384], P(('section', 'wide')), may hold values from 0 to 511
- table: bfloat16 [65536, 8192], P(('section', 'wide'), 'narrow'), may hold values from -51 to 51
- gain: float32 [8192], P('narrow'), may hold values from 0.1 to 1.9
- key_value_weight: bfloat16 [2048, 8192], P(('section', 'wide'), 'narrow'), may hold values from -0.0625 to 0.0625
- kv_target: bfloat16 [16384, 2048], P(('section', 'wide'), 'narrow'), may hold values from -6 to 6
Outputs:
- table_grad: bfloat16 [65536, 8192], P(('section', 'wide'), 'narrow')
Inputs may be any that keep to these rules, and one draw needn't show every extreme that they name: `token_shard`: among the rows of one device, no value is named by more than 2 rows.
All inputs are finite; a program needn't handle non-finite values.
Results may differ from a plain program's by a relative error of at most 0.0056.
Values may be sent and summed in bfloat16 or wider, within the bound.
A program may use at most 64 MiB of HBM per device.

v0:
```python
import jax
import jax.numpy as jnp
from jax import lax
from jax.sharding import PartitionSpec as P

D = 8192
EPSILON = 1e-05


def contract_last(left, right):
    return lax.dot_general(
        left, right, (((1,), (1,)), ((), ())), preferred_element_type=jnp.float32
    )


def on_device(token_shard, token_row, table, gain, key_value_weight, kv_target):
    tokens_here = token_row.shape[0]
    owners = lax.axis_size(("section", "wide"))
    slot_count = 2 * tokens_here // owners
    width_here = table.shape[1]
    shard_of = token_shard[:, 0]
    membership = (shard_of[:, None] == jnp.arange(owners, dtype=jnp.int32)[None, :]).astype(
        jnp.int32
    )
    ranking = jnp.sum((jnp.cumsum(membership, axis=0) - 1) * membership, axis=1)
    position = shard_of * slot_count + ranking
    requests = (
        jnp.full((owners * slot_count,), -1, jnp.int32)
        .at[position]
        .set(token_row)
        .reshape(owners, slot_count)
    )
    holder = (
        jnp.full((owners * slot_count,), -1, jnp.int32)
        .at[position]
        .set(jnp.arange(tokens_here, dtype=jnp.int32))
    )
    wanted = lax.all_to_all(requests, ("section", "wide"), split_axis=0, concat_axis=0, tiled=True)
    present = wanted >= 0
    picked = jnp.take(table, jnp.where(present, wanted, 0), axis=0)
    returned = lax.all_to_all(
        jnp.where(present[..., None], picked, jnp.zeros((), table.dtype)),
        ("section", "wide"),
        split_axis=0,
        concat_axis=0,
        tiled=True,
    )
    hidden = jnp.take(returned.reshape(owners * slot_count, width_here), position, axis=0)
    rows_float = hidden.astype(jnp.float32)
    mean_square = lax.psum(jnp.sum(rows_float * rows_float, axis=1), "narrow") / D
    row_scale = lax.rsqrt(mean_square + EPSILON)
    normed = (rows_float * row_scale[:, None] * gain[None, :]).astype(jnp.bfloat16)
    weight_full = lax.all_gather(key_value_weight, ("section", "wide"), axis=0, tiled=True)
    partial_value = contract_last(normed, weight_full)
    projected = lax.psum_scatter(partial_value, "narrow", scatter_dimension=1, tiled=True)
    residual = (projected - kv_target.astype(jnp.float32)).astype(jnp.bfloat16)
    residual_full = lax.all_gather(residual, "narrow", axis=1, tiled=True)
    back_rows = jnp.dot(residual_full, weight_full, preferred_element_type=jnp.float32)
    weighted = back_rows * gain[None, :]
    inner_sum = lax.psum(jnp.sum(weighted * rows_float, axis=1), "narrow")
    grad_rows = (
        row_scale[:, None] * weighted - rows_float * (row_scale**3 * inner_sum / D)[:, None]
    ).astype(jnp.bfloat16)
    occupied = holder >= 0
    outgoing = jnp.where(
        occupied[:, None],
        jnp.take(grad_rows, jnp.where(occupied, holder, 0), axis=0),
        jnp.zeros((), jnp.bfloat16),
    )
    incoming = lax.all_to_all(
        outgoing.reshape(owners, slot_count, width_here),
        ("section", "wide"),
        split_axis=0,
        concat_axis=0,
        tiled=True,
    )
    vocab_rows = table.shape[0]
    matches = (
        wanted.reshape(1, owners * slot_count) == jnp.arange(vocab_rows, dtype=jnp.int32)[:, None]
    ).astype(jnp.bfloat16)
    table_grad = jnp.dot(
        matches,
        incoming.reshape(owners * slot_count, width_here),
        preferred_element_type=jnp.float32,
    )
    return table_grad.astype(jnp.bfloat16)


def solution(mesh):
    return jax.shard_map(
        on_device,
        mesh=mesh,
        in_specs=(
            P(("section", "wide"), None),
            P(("section", "wide")),
            P(("section", "wide"), "narrow"),
            P("narrow"),
            P(("section", "wide"), "narrow"),
            P(("section", "wide"), "narrow"),
        ),
        out_specs=P(("section", "wide"), "narrow"),
        check_vma=False,
    )
```

profile of v0, /device:TPU:1, one launch (start us, length us, event | category | flops | bytes accessed | tf_op | source)
XLA Modules:
  0.0 417.6 jit_solution(1082262638751350529)
XLA Ops:
  6.5 0.7 all-gather.2.cloned.1.call-update
  7.3 0.7 fusion.11
  8.2 0.8 select_reduce_fusion
  9.0 0.7 and_bitcast_fusion
  9.7 1.1 scatter_custom_fusion
  10.9 35.0 %all_to_all.25 = s32[128,1,2]{2,1,0:T(1,128)S(1)} all-to-all(s32[128,1,2]{2,1,0:T(1,128)S(1)} %bitcast.20), channel_id=1, replica_groups=mesh['section'=2,'wide'=64,'narrow'=4] {'section','wide'}, dimensions={0} | all-to-all | bytes 2048 | tf_op jit(solution)/shard_map/all_to_all | solution.py:38
  46.1 1.4 gather_fusion
  47.5 1.5 reshape.80
  49.0 3.2 broadcast_select_fusion.1
  52.3 7.8 %all-to-all-start.1 = ((bf16[128,2,2048]{2,1,0:T(2,128)(2,1)}), bf16[128,2,2048]{2,1,0:T(2,128)(2,1)}, u32[]{:S(2)}, u32[]{:S(2)}) async-start(bf16[128,2,2048]{2,1,0:T(2,128)(2,1)} %broadcast_select_fusion.1), calls=%async_computation.1 | async-start | bytes 2097152 | tf_op jit(solution)/shard_map/all_to_all | solution.py:41
  60.2 58.5 %all-to-all-done.1 = bf16[128,2,2048]{2,1,0:T(2,128)(2,1)} async-done(((bf16[128,2,2048]{2,1,0:T(2,128)(2,1)}), bf16[128,2,2048]{2,1,0:T(2,128)(2,1)}, u32[]{:S(2)}, u32[]{:S(2)}) %all-to-all-start.1) | async-done | bytes 1048608 | tf_op jit(solution)/shard_map/all_to_all | solution.py:41
  118.7 1.5 reshape.77
  120.2 1.8 gather_fusion.1
  121.9 1.4 fusion
  123.3 8.5 %psum.14 = f32[128]{0:T(128)S(1)} all-reduce(f32[128]{0:T(128)S(1)} %fusion), channel_id=1, replica_groups=mesh['section'=2,'wide'=64,'narrow'=4] {'narrow'}, use_global_device_ids=true, to_apply=%region_5.6 | all-reduce | flops 128 | bytes 1024 | tf_op jit(solution)/shard_map/psum | solution.py:50
  131.8 129.1 %all-gather.2.cloned.1.call-done = bf16[2048,2048]{1,0:T(8,128)(2,1)} async-done(((bf16[16,2048]{1,0:T(8,128)(2,1)}), bf16[2048,2048]{1,0:T(8,128)(2,1)}) %all-gather.2.cloned.1.call-update) | async-done | bytes 8388624 | tf_op jit(solution)/shard_map/all_gather | solution.py:53
  260.9 7.4 %fusion.6 = f32[128,2048]{1,0:T(8,128)} fusion(bf16[2048,2048]{1,0:T(8,128)(2,1)} %all-gather.2.cloned.1.call-done, f32[2048]{0:T(1024)S(1)} %copy-done.3, f32[128]{0:T(128)S(1)} %add_rsqrt_fusion, bf16[128,2048]{1,0:T(8,128)(2,1)} %gather_fusion.1, pred[128]{0:T(512)(128)(4,1)S(1)} %get-tuple-element.7), kind=kOutput, calls=%fused_computation.21 | convolution fusion | flops 1075052544 | bytes 9970304 | tf_op jit(solution)/shard_map/dot_general | solution.py:11
  268.4 1.0 scatter_custom_fusion.1
  269.7 26.5 %reduce-scatter.2.cloned.1.call-done = f32[128,512]{1,0:T(8,128)} async-done(((f32[128,2048]{1,0:T(8,128)}), f32[128,512]{1,0:T(8,128)}) %reduce-scatter.2.cloned.1.call-update) | async-done | bytes 262160 | tf_op jit(solution)/shard_map/reduce_scatter | solution.py:55
  296.3 1.0 subtract_convert_fusion
  297.3 10.7 %all_gather.7 = bf16[128,2048]{1,0:T(8,128)(2,1)S(1)} all-gather(bf16[128,512]{1,0:T(8,128)(2,1)S(1)} %subtract_convert_fusion), channel_id=1, replica_groups=mesh['section'=2,'wide'=64,'narrow'=4] {'narrow'}, dimensions={1}, use_global_device_ids=true | all-gather | bytes 655360 | tf_op jit(solution)/shard_map/all_gather | solution.py:57
  307.9 5.7 %fusion.3 = (f32[128]{0:T(128)S(1)}, f32[128,2048]{1,0:T(8,128)}) fusion(bf16[128,2048]{1,0:T(8,128)(2,1)S(1)} %copy-done.1, pred[128]{0:T(512)(128)(4,1)S(1)} %get-tuple-element.7, f32[2048]{0:T(1024)S(1)} %copy-done.3, bf16[128,2048]{1,0:T(8,128)(2,1)S(1)} %all_gather.7, bf16[2048,2048]{1,0:T(8,128)(2,1)} %all-gather.2.cloned.1.call-done), kind=kOutput, calls=%fused_computation.18 | convolution fusion | flops 1075052416 | bytes 10494592 | tf_op jit(solution)/shard_map/dot_general | solution.py:58
  313.7 6.0 %psum.15 = f32[128]{0:T(128)S(1)} all-reduce(f32[128]{0:T(128)S(1)} %get-tuple-element.12), channel_id=1, replica_groups=mesh['section'=2,'wide'=64,'narrow'=4] {'narrow'}, use_global_device_ids=true, to_apply=%region_8.9 | all-reduce | flops 128 | bytes 1024 | tf_op jit(solution)/shard_map/psum | solution.py:60
  319.7 1.5 fusion.5
  321.2 2.3 gather_fusion.2
  323.5 1.7 gather.17
  325.3 2.4 broadcast_select_fusion.3
  327.7 23.3 %all-to-all-start.2 = ((bf16[128,2,2048]{2,1,0:T(2,128)(2,1)}), bf16[128,2,2048]{2,1,0:T(2,128)(2,1)S(1)}, u32[]{:S(2)}, u32[]{:S(2)}) async-start(bf16[128,2,2048]{2,1,0:T(2,128)(2,1)} %broadcast_select_fusion.3), calls=%async_computation.3 | async-start | bytes 2097152 | tf_op jit(solution)/shard_map/all_to_all | solution.py:70
  351.5 0.8 reduce.3
  352.5 53.7 %all-to-all-done.2 = bf16[128,2,2048]{2,1,0:T(2,128)(2,1)S(1)} async-done(((bf16[128,2,2048]{2,1,0:T(2,128)(2,1)}), bf16[128,2,2048]{2,1,0:T(2,128)(2,1)S(1)}, u32[]{:S(2)}, u32[]{:S(2)}) %all-to-all-start.2) | async-done | bytes 1048608 | tf_op jit(solution)/shard_map/all_to_all | solution.py:70
  406.3 1.2 reshape.78
  407.5 3.3 convolution_convert_fusion
  (27 shorter events, 1.7 us)
Async XLA Ops:
  6.5 39.6 %copy-start = (bf16[512,2048]{1,0:T(8,128)(2,1)S(1)}, bf16[512,2048]{1,0:T(8,128)(2,1)}, u32[]{:S(2)}) copy-start(bf16[512,2048]{1,0:T(8,128)(2,1)} %param.8) | copy-start | bytes 6291460
  6.5 254.4 %all-gather.2.cloned.1.call-start = ((), (), s32[]{:S(2)}) async-start(), calls=%async_computation.4 | async-start | bytes 8454144 | tf_op jit(solution)/shard_map/all_gather | solution.py:53
  47.5 213.5 %copy-start.3 = (f32[2048]{0:T(1024)S(1)}, f32[2048]{0:T(1024)}, u32[]{:S(2)}) copy-start(f32[2048]{0:T(1024)} %param.9) | copy-start | bytes 24580
  52.3 66.4 %all-to-all-start.1 = ((bf16[128,2,2048]{2,1,0:T(2,128)(2,1)}), bf16[128,2,2048]{2,1,0:T(2,128)(2,1)}, u32[]{:S(2)}, u32[]{:S(2)}) async-start(bf16[128,2,2048]{2,1,0:T(2,128)(2,1)} %broadcast_select_fusion.1), calls=%async_computation.1 | async-start | bytes 2097152 | tf_op jit(solution)/shard_map/all_to_all | solution.py:41
  60.1 236.1 %reduce-scatter.2.cloned.1.call-start = ((), (), s32[]{:S(2)}) async-start(), calls=%async_computation.5 | async-start | bytes 1310720 | tf_op jit(solution)/shard_map/reduce_scatter | solution.py:55
  120.1 176.1 %copy-start.2 = (bf16[128,512]{1,0:T(8,128)(2,1)S(1)}, bf16[128,512]{1,0:T(8,128)(2,1)}, u32[]{:S(2)}) copy-start(bf16[128,512]{1,0:T(8,128)(2,1)} %param.11) | copy-start | bytes 393220
  121.9 186.0 %copy-start.1 = (bf16[128,2048]{1,0:T(8,128)(2,1)S(1)}, bf16[128,2048]{1,0:T(8,128)(2,1)}, u32[]{:S(2)}) copy-start(bf16[128,2048]{1,0:T(8,128)(2,1)} %gather_fusion.1) | copy-start | bytes 1572868
  327.7 78.6 %all-to-all-start.2 = ((bf16[128,2,2048]{2,1,0:T(2,128)(2,1)}), bf16[128,2,2048]{2,1,0:T(2,128)(2,1)S(1)}, u32[]{:S(2)}, u32[]{:S(2)}) async-start(bf16[128,2,2048]{2,1,0:T(2,128)(2,1)} %broadcast_select_fusion.3), calls=%async_computation.3 | async-start | bytes 2097152 | tf_op jit(solution)/shard_map/all_to_all | solution.py:70
Sparse Core Ops, SparseCore 0:
  9.5 251.3 all-gather.1
  268.5 27.6 reduce-scatter.1
where the time goes:
time: 418 us
  waiting for transfers between devices  269 us (64%)
  blocking collectives  60.2 us (14%)
  starting transfers between devices  31.1 us (7%)
  matrix products  16.4 us (4%)
  local copies, waits for them, and re-layouts  14.8 us (4%)
  between operations  13.6 us (3%)
  other arithmetic  12.9 us (3%)
    all_gather x1, waiting for transfers between devices, on_device(): lax.all_gather(key_value_weight, ('section', 'wide'), axis=0, tiled=True)  129 us
    all_to_all x1, waiting for transfers between devices, on_device(): lax.all_to_all(jnp.where(present[..., None], picked, jnp.zeros((), table....  58.5 us
    all_to_all x1, waiting for transfers between devices, on_device(): lax.all_to_all(outgoing.reshape(owners, slot_count, width_here), ('sectio...  53.7 us
    all_to_all x1, blocking collectives, on_device(): lax.all_to_all(requests, ('section', 'wide'), split_axis=0, concat_axis=0...  35 us
    reduce_scatter x1, waiting for transfers between devices, on_device(): lax.psum_scatter(partial_value, 'narrow', scatter_dimension=1, tiled=True)  26.5 us
    all_to_all x1, starting transfers between devices, on_device(): lax.all_to_all(outgoing.reshape(owners, slot_count, width_here), ('sectio...  23.3 us
    all_gather x1, blocking collectives, on_device(): residual_full = lax.all_gather(residual, 'narrow', axis=1, tiled=True)  10.7 us
    psum x1, blocking collectives, on_device(): lax.psum(jnp.sum(rows_float * rows_float, axis=1), 'narrow') / D  8.48 us
  transfers between devices with their start and end apart: 4, of which 4 were waited for; matrix products, arithmetic and copies ran while one was open for 4% of the time, Pallas kernels for 0%

commit v1 on v0

--- a/solution.py
+++ b/solution.py
@@ -50,7 +50,15 @@
     mean_square = lax.psum(jnp.sum(rows_float * rows_float, axis=1), "narrow") / D
     row_scale = lax.rsqrt(mean_square + EPSILON)
     normed = (rows_float * row_scale[:, None] * gain[None, :]).astype(jnp.bfloat16)
-    weight_full = lax.all_gather(key_value_weight, ("section", "wide"), axis=0, tiled=True)
+    weight_full = jnp.concatenate(
+        lax.all_to_all(
+            jnp.stack([key_value_weight] * lax.axis_size(("section", "wide"))),
+            ("section", "wide"),
+            0,
+            0,
+        ),
+        axis=0,
+    )
     partial_value = contract_last(normed, weight_full)
     projected = lax.psum_scatter(partial_value, "narrow", scatter_dimension=1, tiled=True)
     residual = (projected - kv_target.astype(jnp.float32)).astype(jnp.bfloat16)

time: 418 us -> 645 us (1.54)
  waiting for transfers between devices: 269 us -> 429 us
  blocking collectives: 60.2 us -> 123 us
    all_to_all x1, waiting for transfers between devices: 58.5 us -> 351 us  [on_device(): lax.all_to_all(jnp.stack([key_value_weight] * lax.axis_size(('section', '...]
    all_gather x1 -> x0, waiting for transfers between devices: 129 us -> none  [on_device(): lax.all_gather(key_value_weight, ('section', 'wide'), axis=0, tiled=True)]
    all_to_all x0 -> x1, blocking collectives: none -> 61.6 us  [on_device(): lax.all_to_all(jnp.where(present[..., None], picked, jnp.zeros((), table....]
  transfers between devices with their start and end apart: 4 -> 3, of which waited for: 4 -> 3; matrix products, arithmetic and copies ran while one was open for 4% -> 1% of each run, Pallas kernels for 0% -> 0%
where the time goes in v1:
time: 645 us
  waiting for transfers between devices  429 us (67%)
  blocking collectives  123 us (19%)
  starting transfers between devices  31.3 us (5%)
  local copies, waits for them, and re-layouts  19 us (3%)
  matrix products  16.4 us (3%)
  between operations  13.6 us (2%)
  other arithmetic  12.2 us (2%)
    all_to_all x1, waiting for transfers between devices, on_device(): lax.all_to_all(jnp.stack([key_value_weight] * lax.axis_size(('section', '...  351 us
    all_to_all x1, blocking collectives, on_device(): lax.all_to_all(jnp.where(present[..., None], picked, jnp.zeros((), table....  61.6 us
    all_to_all x1, waiting for transfers between devices, on_device(): lax.all_to_all(outgoing.reshape(owners, slot_count, width_here), ('sectio...  53.7 us
    all_to_all x1, blocking collectives, on_device(): lax.all_to_all(requests, ('section', 'wide'), split_axis=0, concat_axis=0...  35 us
    reduce_scatter x1, waiting for transfers between devices, on_device(): lax.psum_scatter(partial_value, 'narrow', scatter_dimension=1, tiled=True)  24.6 us
    all_to_all x1, starting transfers between devices, on_device(): lax.all_to_all(outgoing.reshape(owners, slot_count, width_here), ('sectio...  23.3 us
  transfers between devices with their start and end apart: 3, of which 3 were waited for; matrix products, arithmetic and copies ran while one was open for 1% of the time, Pallas kernels for 0%

profile of v1, /device:TPU:1, one launch (start us, length us, event | category | flops | bytes accessed | tf_op | source)
XLA Modules:
  0.0 644.7 jit_solution(306322877704074395)
XLA Ops:
  6.5 0.9 fusion.11
  7.6 0.8 select_reduce_fusion
  8.4 0.7 and_bitcast_fusion
  9.1 1.1 scatter_custom_fusion
  10.4 35.0 %all_to_all.30 = s32[128,1,2]{2,1,0:T(1,128)S(1)} all-to-all(s32[128,1,2]{2,1,0:T(1,128)S(1)} %bitcast.23), channel_id=1, replica_groups=mesh['section'=2,'wide'=64,'narrow'=4] {'section','wide'}, dimensions={0} | all-to-all | bytes 2048 | tf_op jit(solution)/shard_map/all_to_all | solution.py:38
  45.6 1.4 gather_fusion
  46.9 1.5 reshape.86
  48.4 2.5 broadcast_select_fusion.1
  50.9 61.6 %all_to_all.31 = bf16[128,2,2048]{2,1,0:T(2,128)(2,1)} all-to-all(bf16[128,2,2048]{2,1,0:T(2,128)(2,1)S(1)} %broadcast_select_fusion.1), channel_id=1, replica_groups=mesh['section'=2,'wide'=64,'narrow'=4] {'section','wide'}, dimensions={0} | all-to-all | bytes 2097152 | tf_op jit(solution)/shard_map/all_to_all | solution.py:41
  112.5 4.3 stack.2
  116.8 8.0 %all-to-all-start.2 = ((bf16[128,16,2048]{2,1,0:T(8,128)(2,1)}), bf16[128,16,2048]{2,1,0:T(8,128)(2,1)}, u32[]{:S(2)}, u32[]{:S(2)}) async-start(bf16[128,16,2048]{2,1,0:T(8,128)(2,1)} %stack.2), calls=%async_computation.2 | async-start | bytes 16777216 | tf_op jit(solution)/shard_map/all_to_all | solution.py:54
  124.8 1.5 reshape.82
  126.3 1.7 gather_fusion.1
  128.1 1.4 fusion
  129.5 9.4 %psum.14 = f32[128]{0:T(128)S(1)} all-reduce(f32[128]{0:T(128)S(1)} %fusion), channel_id=1, replica_groups=mesh['section'=2,'wide'=64,'narrow'=4] {'narrow'}, use_global_device_ids=true, to_apply=%region_5.6 | all-reduce | flops 128 | bytes 1024 | tf_op jit(solution)/shard_map/psum | solution.py:50
  138.9 351.1 %all-to-all-done.2 = bf16[128,16,2048]{2,1,0:T(8,128)(2,1)} async-done(((bf16[128,16,2048]{2,1,0:T(8,128)(2,1)}), bf16[128,16,2048]{2,1,0:T(8,128)(2,1)}, u32[]{:S(2)}, u32[]{:S(2)}) %all-to-all-start.2) | async-done | bytes 8388640 | tf_op jit(solution)/shard_map/all_to_all | solution.py:54
  490.0 7.4 %fusion.6 = f32[128,2048]{1,0:T(8,128)} fusion(bf16[2048,2048]{1,0:T(8,128)(2,1)} %bitcast.7, f32[2048]{0:T(1024)S(1)} %copy-done.4, f32[128]{0:T(128)S(1)} %add_rsqrt_fusion, bf16[128,2048]{1,0:T(8,128)(2,1)} %gather_fusion.1, pred[128]{0:T(512)(128)(4,1)S(1)} %get-tuple-element.7), kind=kOutput, calls=%fused_computation.21 | convolution fusion | flops 1075052544 | bytes 9970304 | tf_op jit(solution)/shard_map/dot_general | solution.py:11
  497.5 1.0 scatter_custom_fusion.1
  498.8 24.6 %reduce-scatter.2.cloned.1.call-done = f32[128,512]{1,0:T(8,128)} async-done(((f32[128,2048]{1,0:T(8,128)}), f32[128,512]{1,0:T(8,128)}) %reduce-scatter.2.cloned.1.call-update) | async-done | bytes 262160 | tf_op jit(solution)/shard_map/reduce_scatter | solution.py:63
  523.4 1.0 subtract_convert_fusion
  524.4 10.7 %all_gather.3 = bf16[128,2048]{1,0:T(8,128)(2,1)S(1)} all-gather(bf16[128,512]{1,0:T(8,128)(2,1)S(1)} %subtract_convert_fusion), channel_id=1, replica_groups=mesh['section'=2,'wide'=64,'narrow'=4] {'narrow'}, dimensions={1}, use_global_device_ids=true | all-gather | bytes 655360 | tf_op jit(solution)/shard_map/all_gather | solution.py:65
  535.1 5.7 fusion.3
  540.8 6.0 psum.15
  546.8 1.5 fusion.5
  548.3 2.3 gather_fusion.2
  550.6 1.7 gather.17
  552.4 2.4 broadcast_select_fusion.3
  554.8 23.3 %all-to-all-start.3 = ((bf16[128,2,2048]{2,1,0:T(2,128)(2,1)}), bf16[128,2,2048]{2,1,0:T(2,128)(2,1)S(1)}, u32[]{:S(2)}, u32[]{:S(2)}) async-start(bf16[128,2,2048]{2,1,0:T(2,128)(2,1)} %broadcast_select_fusion.3), calls=%async_computation.4 | async-start | bytes 2097152 | tf_op jit(solution)/shard_map/all_to_all | solution.py:78
  578.7 0.8 reduce.3
  579.7 53.7 %all-to-all-done.3 = bf16[128,2,2048]{2,1,0:T(2,128)(2,1)S(1)} async-done(((bf16[128,2,2048]{2,1,0:T(2,128)(2,1)}), bf16[128,2,2048]{2,1,0:T(2,128)(2,1)S(1)}, u32[]{:S(2)}, u32[]{:S(2)}) %all-to-all-start.3) | async-done | bytes 1048608 | tf_op jit(solution)/shard_map/all_to_all | solution.py:78
  633.4 1.2 reshape.84
  634.6 3.3 convolution_convert_fusion
  (28 shorter events, 1.7 us)
Async XLA Ops:
  6.5 39.0 %copy-start = (bf16[512,2048]{1,0:T(8,128)(2,1)S(1)}, bf16[512,2048]{1,0:T(8,128)(2,1)}, u32[]{:S(2)}) copy-start(bf16[512,2048]{1,0:T(8,128)(2,1)} %param.8) | copy-start | bytes 6291460
  6.5 106.0 %copy-start.3 = (bf16[16,2048]{1,0:T(8,128)(2,1)S(1)}, bf16[16,2048]{1,0:T(8,128)(2,1)}, u32[]{:S(2)}) copy-start(bf16[16,2048]{1,0:T(8,128)(2,1)} %param.10) | copy-start | bytes 196612
  116.8 373.2 %copy-start.4 = (f32[2048]{0:T(1024)S(1)}, f32[2048]{0:T(1024)}, u32[]{:S(2)}) copy-start(f32[2048]{0:T(1024)} %param.9) | copy-start | bytes 24580
  116.8 373.2 %all-to-all-start.2 = ((bf16[128,16,2048]{2,1,0:T(8,128)(2,1)}), bf16[128,16,2048]{2,1,0:T(8,128)(2,1)}, u32[]{:S(2)}, u32[]{:S(2)}) async-start(bf16[128,16,2048]{2,1,0:T(8,128)(2,1)} %stack.2), calls=%async_computation.2 | async-start | bytes 16777216 | tf_op jit(solution)/shard_map/all_to_all | solution.py:54
  124.8 398.6 %reduce-scatter.2.cloned.1.call-start = ((), (), s32[]{:S(2)}) async-start(), calls=%async_computation.5 | async-start | bytes 1310720 | tf_op jit(solution)/shard_map/reduce_scatter | solution.py:63
  126.3 397.1 %copy-start.2 = (bf16[128,512]{1,0:T(8,128)(2,1)S(1)}, bf16[128,512]{1,0:T(8,128)(2,1)}, u32[]{:S(2)}) copy-start(bf16[128,512]{1,0:T(8,128)(2,1)} %param.11) | copy-start | bytes 393220
  128.1 407.0 %copy-start.1 = (bf16[128,2048]{1,0:T(8,128)(2,1)S(1)}, bf16[128,2048]{1,0:T(8,128)(2,1)}, u32[]{:S(2)}) copy-start(bf16[128,2048]{1,0:T(8,128)(2,1)} %gather_fusion.1) | copy-start | bytes 1572868
  554.8 78.6 %all-to-all-start.3 = ((bf16[128,2,2048]{2,1,0:T(2,128)(2,1)}), bf16[128,2,2048]{2,1,0:T(2,128)(2,1)S(1)}, u32[]{:S(2)}, u32[]{:S(2)}) async-start(bf16[128,2,2048]{2,1,0:T(2,128)(2,1)} %broadcast_select_fusion.3), calls=%async_computation.4 | async-start | bytes 2097152 | tf_op jit(solution)/shard_map/all_to_all | solution.py:78
Sparse Core Ops, SparseCore 0:
  497.6 25.7 reduce-scatter.1
